TPU v7x, 32 devices: a whole 2x2x4 slice. The times are simulated.
32 devices in a mesh: col: 4 (over y, x), bulk: 8 (over z, core).
Axes of the slice: x: 2, y: 2, z: 4, core: 2. Of those that a mesh axis runs over, the one named last changes fastest.
Arguments:
- sequence_embedding: bfloat16 [64, 128, 64], P('bulk', 'col'), may hold values from -6 to 6
- residue_couplings: bfloat16 [128, 128, 128], P('bulk', 'col'), may hold values from -6 to 6
- sequence_layernorm_factor: float32 [64], replicated, may hold values from 0.5 to 1.5
- coupling_layernorm_factor: float32 [128], replicated, may hold values from 0.5 to 1.5
- content_projection: bfloat16 [64, 256], replicated, may hold values from -0.75 to 0.75
- switch_projection: bfloat16 [64, 256], replicated, may hold values from -0.75 to 0.75
- attention_score_projection: bfloat16 [128, 8], replicated, may hold values from -0.29882812 to 0.29882812
- final_projection: bfloat16 [256, 64], replicated, may hold values from -2 to 2
- residual_change_cotangent: bfloat16 [64, 128, 64], P('bulk', 'col'), may hold values from -6 to 6
Outputs:
- residual_change: bfloat16 [64, 128, 64], P('bulk', 'col')
- sequence_embedding_sensitivity: bfloat16 [64, 128, 64], P('bulk', 'col')
- coupling_sensitivity: bfloat16 [128, 128, 128], P('bulk', 'col')
All inputs are finite; a program needn't handle non-finite values.
Results may differ from a plain program's by a relative error of at most 0.025.
Values may be sent and summed in bfloat16 or wider, within the bound.
A program may use at most 64 MiB of HBM per device.

v0:
```python
import jax
import jax.numpy as jnp
from jax import lax
from jax.sharding import PartitionSpec as P

epsilon = 1e-05


def centred_sequences(inputs, scale_gain):
    widened = inputs.astype(jnp.float32)
    row_mean = jnp.mean(widened, axis=-1, keepdims=True)
    centered = widened - row_mean
    variance = jnp.mean(centered * centered, axis=-1, keepdims=True)
    inv_std = lax.rsqrt(variance + epsilon)
    normed = centered * inv_std
    return (normed * scale_gain, normed, inv_std)


def layernorm_reverse_mode(upstream, normed, inv_std, scale_gain):
    scaled = upstream * scale_gain
    mean_grad = jnp.mean(scaled, axis=-1, keepdims=True)
    mean_proj = jnp.mean(scaled * normed, axis=-1, keepdims=True)
    return inv_std * (scaled - mean_grad - normed * mean_proj)


def per_device(
    sequence_embedding,
    residue_couplings,
    sequence_layernorm_factor,
    coupling_layernorm_factor,
    content_projection,
    switch_projection,
    attention_score_projection,
    final_projection,
    residual_change_cotangent,
):
    number_of_heads = attention_score_projection.shape[1]
    value_channels = content_projection.shape[1]
    head_channels = value_channels // number_of_heads
    device_sequences = sequence_embedding.shape[0]
    device_residues = sequence_embedding.shape[1]
    finest_accuracy = lax.Precision.HIGHEST
    out_wide = final_projection.astype(jnp.float32)
    switch_single_form = switch_projection.astype(jnp.float32)
    bias_wide = attention_score_projection.astype(jnp.float32)
    pair_scaled, pair_hat, pair_inv = centred_sequences(
        residue_couplings, coupling_layernorm_factor
    )
    logits = jnp.einsum(
        "ijk,kh->hij",
        pair_scaled.astype(jnp.bfloat16),
        attention_score_projection,
        preferred_element_type=jnp.float32,
    )
    exponent = jnp.exp(logits)
    totals = lax.psum(jnp.sum(exponent, axis=2), "col")
    weights = exponent / totals[:, :, None]
    weights_low = weights.astype(jnp.bfloat16)
    weight_panel = lax.all_gather(weights_low, "bulk", axis=1, tiled=True)
    all_tokens = weight_panel.shape[1]
    sequence_scaled_by_factor, sequence_centred_unit, sequence_reciprocal_spread = (
        centred_sequences(sequence_embedding, sequence_layernorm_factor)
    )
    sequence_embedding_brief = sequence_scaled_by_factor.astype(jnp.bfloat16)
    content_sequences = jnp.dot(
        sequence_embedding_brief, content_projection, preferred_element_type=jnp.float32
    ).astype(jnp.bfloat16)
    value_per_head = content_sequences.reshape(
        device_sequences, device_residues, number_of_heads, head_channels
    )
    partial_value = jnp.einsum(
        "hij,sjhc->sihc", weight_panel, value_per_head, preferred_element_type=jnp.float32
    ).reshape(device_sequences, all_tokens, value_channels)
    partial_low = partial_value.astype(jnp.bfloat16)
    sigmoid_switch = jax.nn.sigmoid(
        jnp.dot(sequence_embedding_brief, switch_projection, preferred_element_type=jnp.float32)
    )
    pair_average = lax.psum_scatter(partial_low, "col", scatter_dimension=1, tiled=True).astype(
        jnp.float32
    )
    residual_change = jnp.dot(
        sigmoid_switch * pair_average, out_wide, precision=finest_accuracy
    ).astype(jnp.bfloat16)
    d_gated = jnp.dot(
        residual_change_cotangent.astype(jnp.float32), out_wide.T, precision=finest_accuracy
    )
    d_average_here = (sigmoid_switch * d_gated).astype(jnp.bfloat16)
    average_gradient = lax.all_gather(d_average_here, "col", axis=1, tiled=True)
    switch_preimage_sensitivity = d_gated * pair_average * sigmoid_switch * (1.0 - sigmoid_switch)
    gate_contribution = jnp.dot(
        switch_preimage_sensitivity, switch_single_form.T, precision=finest_accuracy
    )
    head_gradient = average_gradient.reshape(
        device_sequences, all_tokens, number_of_heads, head_channels
    )
    content_sensitivity = jnp.einsum(
        "hij,sihc->sjhc", weight_panel, head_gradient, preferred_element_type=jnp.float32
    )
    content_sensitivity = content_sensitivity.reshape(
        device_sequences, device_residues, value_channels
    ).astype(jnp.bfloat16)
    weight_part = jnp.einsum(
        "sihc,sjhc->hij", head_gradient, value_per_head, preferred_element_type=jnp.float32
    )
    d_weights = lax.psum_scatter(
        weight_part.astype(jnp.bfloat16), "bulk", scatter_dimension=1, tiled=True
    ).astype(jnp.float32)
    row_dot = lax.psum(jnp.sum(weights_low.astype(jnp.float32) * d_weights, axis=2), "col")
    d_logits = weights * (d_weights - row_dot[:, :, None])
    d_pair_low = jnp.einsum("hij,kh->ijk", d_logits, bias_wide, precision=finest_accuracy)
    coupling_sensitivity = layernorm_reverse_mode(
        d_pair_low, pair_hat, pair_inv, coupling_layernorm_factor
    ).astype(jnp.bfloat16)
    sequence_sensitivity_brief = (
        jnp.dot(content_sensitivity, content_projection.T, preferred_element_type=jnp.float32)
        + gate_contribution
    )
    sequence_embedding_sensitivity = layernorm_reverse_mode(
        sequence_sensitivity_brief,
        sequence_centred_unit,
        sequence_reciprocal_spread,
        sequence_layernorm_factor,
    ).astype(jnp.bfloat16)
    return (residual_change, sequence_embedding_sensitivity, coupling_sensitivity)


def solution(mesh):
    in_specs = (
        P("bulk", "col", None),
        P("bulk", "col", None),
        P(),
        P(),
        P(),
        P(),
        P(),
        P(),
        P("bulk", "col", None),
    )
    out_specs = (P("bulk", "col", None), P("bulk", "col", None), P("bulk", "col", None))
    return jax.shard_map(
        per_device, mesh=mesh, in_specs=in_specs, out_specs=out_specs, check_vma=False
    )
```

profile of v0, /device:TPU:0, one launch (start us, length us, event | category | flops | bytes accessed | tf_op | source)
XLA Modules:
  0.0 105.6 jit_solution(678878752773036502)
XLA Ops:
  7.2 1.0 convert_reduce_fusion.1
  8.5 0.5 copy-done.4
  9.6 0.5 copy-done.5
  10.3 0.6 copy-done.6
  11.2 11.5 %all_gather.7 = bf16[8,128,256]{2,1,0:T(8,128)(2,1)S(1)} all-gather(bf16[8,32,256]{2,1,0:T(8,128)(2,1)S(1)} %get-tuple-element.9), channel_id=1, replica_groups=mesh['col'=4,'bulk'=8] {'col'}, dimensions={1}, use_global_device_ids=true | all-gather | bytes 655360 | tf_op jit(solution)/shard_map/all_gather | solution.py:88
  23.3 0.9 copy.64
  24.3 0.8 copy-done.2
  25.5 0.6 copy-done.9
  26.2 0.4 fusion.65
  26.6 9.1 %psum.14 = f32[8,16]{0,1:T(8,128)S(1)} all-reduce(f32[8,16]{0,1:T(8,128)S(1)} %get-tuple-element.11), channel_id=1, replica_groups=mesh['col'=4,'bulk'=8] {'col'}, use_global_device_ids=true, to_apply=%region_5.0 | all-reduce | flops 128 | bytes 1024 | tf_op jit(solution)/shard_map/psum | solution.py:56
  35.7 19.7 %reduce-scatter.5.cloned.1.call-done = bf16[8,16,32]{2,0,1:T(8,128)(2,1)} async-done(((bf16[8,128,32]{2,0,1:T(8,128)(2,1)}), bf16[8,16,32]{2,0,1:T(8,128)(2,1)}) %reduce-scatter.5.cloned.1.call-update) | async-done | bytes 8208 | tf_op jit(solution)/shard_map/reduce_scatter | solution.py:105
  55.4 0.9 fusion.45
  56.3 14.2 %all_gather.6 = bf16[8,128,32]{2,0,1:T(8,128)(2,1)S(1)} all-gather(bf16[8,16,32]{2,0,1:T(8,128)(2,1)S(1)} %get-tuple-element.8), channel_id=1, replica_groups=mesh['col'=4,'bulk'=8] {'bulk'}, dimensions={1}, use_global_device_ids=true | all-gather | bytes 73728 | tf_op jit(solution)/shard_map/all_gather | solution.py:59
  70.5 0.4 fusion
  70.9 1.0 copy.57
  72.2 0.3 copy.61
  72.6 0.4 convert_element_type.78
  73.0 10.5 %psum.15 = f32[8,16]{0,1:T(8,128)S(1)} all-reduce(f32[8,16]{0,1:T(8,128)S(1)} %get-tuple-element.7), channel_id=1, replica_groups=mesh['col'=4,'bulk'=8] {'col'}, use_global_device_ids=true, to_apply=%region_11.0 | all-reduce | flops 128 | bytes 1024 | tf_op jit(solution)/shard_map/psum | solution.py:108
  83.4 0.7 fusion.62
  84.1 1.0 fusion.20
  85.1 10.4 %reduce-scatter.3.cloned.1.call-done = bf16[8,32,256]{2,1,0:T(8,128)(2,1)} async-done(((bf16[8,128,256]{2,1,0:T(8,128)(2,1)}), bf16[8,32,256]{2,1,0:T(8,128)(2,1)}) %reduce-scatter.3.cloned.1.call-update) | async-done | bytes 131088 | tf_op jit(solution)/shard_map/reduce_scatter | solution.py:78
  95.5 1.2 %fusion.24 = f32[8,32,64]{2,1,0:T(8,128)S(1)} fusion(f32[8,32,256]{2,1,0:T(8,128)S(1)} %get-tuple-element.10, f32[8,32,256]{2,1,0:T(8,128)S(1)} %fusion.50, bf16[8,32,256]{2,1,0:T(8,128)(2,1)} %reduce-scatter.3.cloned.1.call-done, bf16[64,256]{1,0:T(8,128)(2,1)S(1)} %copy-done.6), kind=kOutput, calls=%fused_computation.37 | convolution fusion | flops 50659328 | bytes 753664 | tf_op jit(solution)/shard_map/dot_general | solution.py:90
  97.0 0.8 fusion.38
  97.9 0.9 convolution_convert_fusion.3
  (39 shorter events, 3.1 us)
Async XLA Ops:
  7.2 2.4 %copy-start = (bf16[8,32,64]{2,1,0:T(8,128)(2,1)S(1)}, bf16[8,32,64]{2,1,0:T(8,128)(2,1)}, u32[]{:S(2)}) copy-start(bf16[8,32,64]{2,1,0:T(8,128)(2,1)} %param.17) | copy-start | bytes 98308
  7.2 1.0 copy-start.1
  7.2 48.2 %reduce-scatter.5.cloned.1.call-start = ((), (), s32[]{:S(2)}) async-start(), calls=%async_computation.3 | async-start | bytes 294912 | tf_op jit(solution)/shard_map/reduce_scatter | solution.py:105
  8.2 0.8 copy-start.4
  8.4 0.7 copy-start.8
  9.4 0.8 copy-start.5
  10.1 0.8 copy-start.6
  24.2 0.9 copy-start.2
  24.2 71.3 %reduce-scatter.3.cloned.1.call-start = ((), (), s32[]{:S(2)}) async-start(), calls=%async_computation.2 | async-start | bytes 655360 | tf_op jit(solution)/shard_map/reduce_scatter | solution.py:78
  25.5 0.7 copy-start.9
  25.5 0.7 copy-start.10
  72.6 10.8 %copy-start.7 = (bf16[8,16,32]{2,0,1:T(8,128)(2,1)S(1)}, bf16[8,16,32]{2,0,1:T(8,128)(2,1)}, u32[]{:S(2)}) copy-start(bf16[8,16,32]{2,0,1:T(8,128)(2,1)} %reduce-scatter.5.cloned.1.call-done) | copy-start | bytes 24580
  97.0 0.9 copy-start.3
Sparse Core Ops, SparseCore 0:
  24.3 31.0 reduce-scatter.4
  72.1 23.4 reduce-scatter.2
where the time goes:
time: 106 us
  blocking collectives  45.3 us (43%)
  waiting for transfers between devices  30.1 us (28%)
  between operations  14.3 us (13%)
  local copies, waits for them, and re-layouts  6.44 us (6%)
  matrix products  5.12 us (5%)
  other arithmetic  4.33 us (4%)
    reduce_scatter x1, waiting for transfers between devices, per_device(): lax.psum_scatter(weight_part.astype(jnp.bfloat16), 'bulk', scatter_dimens...  19.7 us
    all_gather x1, blocking collectives, per_device(): weight_panel = lax.all_gather(weights_low, 'bulk', axis=1, tiled=True)  14.2 us
    all_gather x1, blocking collectives, per_device(): average_gradient = lax.all_gather(d_average_here, 'col', axis=1, tiled=True)  11.5 us
    psum x1, blocking collectives, per_device(): lax.psum(jnp.sum(weights_low.astype(jnp.float32) * d_weights, axis=2), 'c...  10.5 us
    reduce_scatter x1, waiting for transfers between devices, per_device(): lax.psum_scatter(partial_low, 'col', scatter_dimension=1, tiled=True)  10.4 us
    psum x1, blocking collectives, per_device(): totals = lax.psum(jnp.sum(exponent, axis=2), 'col')  9.09 us
    unnamed x22, local copies, waits for them, and re-layouts  3.31 us
  transfers between devices with their start and end apart: 2, of which 2 were waited for; matrix products, arithmetic and copies ran while one was open for 3% of the time, Pallas kernels for 0%

commit v1 on v0

v1 whole, which is shorter than its diff:
```python
import functools

import jax
import jax.numpy as jnp
from jax import lax
from jax.experimental import pallas as pl
from jax.experimental.pallas import tpu as pltpu
from jax.sharding import PartitionSpec as P

EPS = 1e-05
LANES = 128
MESH = pl.DeviceIdType.MESH
f32 = jnp.float32
bf16 = jnp.bfloat16


def dot(a, b):
    return jnp.dot(a, b, preferred_element_type=f32)


def dot_nt(a, b):
    return lax.dot_general(a, b, (((1,), (1,)), ((), ())), preferred_element_type=f32)


def dot_tn(a, b):
    return lax.dot_general(a, b, (((0,), (0,)), ((), ())), preferred_element_type=f32)


def normed_rows(x):
    centered = x - jnp.mean(x, axis=-1, keepdims=True)
    inv = lax.rsqrt(jnp.mean(centered * centered, axis=-1, keepdims=True) + EPS)
    return centered * inv, inv


def rows_backward(up, hat, inv, gain):
    q = up * gain
    mean_q = jnp.mean(q, axis=-1, keepdims=True)
    mean_p = jnp.mean(q * hat, axis=-1, keepdims=True)
    return inv * (q - mean_q - hat * mean_p)


def split_dot(a, b):
    high = a.astype(bf16)
    low = (a - high.astype(f32)).astype(bf16)
    return dot(high, b) + dot(low, b)


def loop(n, body):
    if n <= 8:
        for k in range(n):
            body(k)
    else:
        lax.fori_loop(0, n, lambda k, _: (body(k), 0)[1], 0)


def kernel(
    nc, nb, ns, nt, ni, nh,
    msa_ref, pair_ref, mgain_ref, pgain_ref, wv_ref, wg_ref, att_ref, wo_ref, cot_ref,
    res_ref, dmsa_ref, dpair_ref,
    x_all, e_all, bd, da, gate_s, dg_s, dw_s, inv_t, avg_s, dv_s, hat_s, rinv_s,
    phat_s, prinv_s, wvg, wop, rep, e_own, d_send, d_recv,
    xs_sem, xr_sem, es_sem, er_sem, ds_sem, dr_sem,
):
    c = lax.axis_index("col")
    b = lax.axis_index("bulk")
    depth = msa_ref.shape[1]
    chans = wv_ref.shape[1]
    tiles = chans // LANES
    hd = chans // nh
    per = LANES // hd
    n = nc * nt

    barrier = pltpu.get_barrier_semaphore()

    def greet(k, _):
        c2 = lax.rem(c + lax.div(k, nb), nc)
        b2 = lax.rem(b + lax.rem(k, nb), nb)
        pl.semaphore_signal(barrier, inc=1, device_id=(c2, b2), device_id_type=MESH)
        return 0

    lax.fori_loop(1, nc * nb, greet, 0)

    mgain = mgain_ref[...]
    pgain = pgain_ref[...]
    hat, rinv = normed_rows(msa_ref[...].astype(f32))
    hat_s[...] = hat
    rinv_s[...] = rinv
    x_all[c, :, :depth] = (hat * mgain).astype(bf16)
    x_all[c, :, depth:] = cot_ref[...]

    pl.semaphore_wait(barrier, nc * nb - 1)

    def x_copy(k):
        c2 = lax.rem(c + k, nc)
        return pltpu.make_async_remote_copy(
            src_ref=x_all.at[c], dst_ref=x_all.at[c],
            send_sem=xs_sem.at[k], recv_sem=xr_sem.at[c],
            device_id=(c2, b), device_id_type=MESH,
        )

    loop(nc - 1, lambda k: x_copy(k + 1).start())

    lane = lax.broadcasted_iota(jnp.int32, (nt, chans), 1)
    row = lax.broadcasted_iota(jnp.int32, (nt, chans), 0)
    same_j = (lax.rem(lane, nt) == row).astype(f32)
    spread = (
        lax.div(lax.broadcasted_iota(jnp.int32, (nh, chans), 1), nt)
        == lax.broadcasted_iota(jnp.int32, (nh, chans), 0)
    ).astype(bf16)
    rep[...] = dot(att_ref[...], spread).astype(bf16)
    phat, prinv = normed_rows(pair_ref[...].astype(f32))
    phat_s[...] = phat
    prinv_s[...] = prinv
    many = dot((phat * pgain).astype(bf16), rep[...])
    logits = jnp.sum(many.reshape(ni, nt, chans) * same_j[None], axis=1)
    e = jnp.exp(logits)
    e_own[...] = e
    my_rows = pl.ds(pl.multiple_of(b * ni, ni), ni)
    e_all[c, my_rows, :] = e.astype(bf16)

    def e_copy(k, send):
        c2 = lax.rem(c + lax.div(k, nb), nc)
        b2 = lax.rem(b + lax.rem(k, nb), nb)
        if send:
            block = e_all.at[c, my_rows]
            slot = er_sem.at[c * nb + b]
        else:
            block = e_all.at[c2, pl.ds(pl.multiple_of(b2 * ni, ni), ni)]
            slot = er_sem.at[c2 * nb + b2]
        return pltpu.make_async_remote_copy(
            src_ref=block, dst_ref=block, send_sem=es_sem.at[k], recv_sem=slot,
            device_id=(c2, b2), device_id_type=MESH,
        )

    def e_start(k, _):
        e_copy(k, True).start()
        return 0

    lax.fori_loop(1, nc * nb, e_start, 0)

    wvg[:depth, :chans] = wv_ref[...]
    wvg[:depth, chans:] = wg_ref[...]
    wvg[depth:, :] = jnp.zeros((depth, 2 * chans), bf16)
    wop[:, :depth] = jnp.zeros((chans, depth), bf16)
    wop[:, depth:] = wo_ref[...]

    head_of = lax.div(lax.broadcasted_iota(jnp.int32, (nt, LANES), 1), hd)
    head_masks = [(head_of == h).astype(f32).astype(bf16) for h in range(per)]

    def chunk(k):
        c2 = lax.rem(c + k, nc)
        if not (isinstance(k, int) and k == 0):
            block = x_all.at[c2]
            pltpu.make_async_remote_copy(
                src_ref=block, dst_ref=block, send_sem=xs_sem.at[k], recv_sem=xr_sem.at[c2],
                device_id=(c2, b), device_id_type=MESH,
            ).wait_recv()
        x = x_all[c2]
        both = dot(x, wvg[...])
        values = both[:, :chans].astype(bf16)
        gate = 1.0 / (1.0 + jnp.exp(-both[:, chans:]))
        dg = dot_nt(x, wop[...])
        dav = (gate * dg).astype(bf16)
        if isinstance(k, int) and k == 0:
            gate_s[...] = gate
            dg_s[...] = dg
        rows = pl.ds(pl.multiple_of(c2 * nt, nt), nt)
        for s in range(ns):
            for t in range(tiles):
                cut = (slice(s * nt, (s + 1) * nt), slice(t * LANES, (t + 1) * LANES))
                da[t, rows, s * LANES:(s + 1) * LANES] = dav[cut]
                piece = values[cut]
                for h in range(per):
                    bd[c2, t, h * nt:(h + 1) * nt, s * LANES:(s + 1) * LANES] = piece * head_masks[h]

    chunk(0)
    loop(nc - 1, lambda k: chunk(k + 1))

    def e_wait(k, _):
        e_copy(k, False).wait_recv()
        return 0

    lax.fori_loop(1, nc * nb, e_wait, 0)

    group = (
        lax.div(lax.broadcasted_iota(jnp.int32, (LANES, LANES), 1), hd)
        == lax.div(lax.broadcasted_iota(jnp.int32, (LANES, LANES), 0), hd)
    ).astype(f32).astype(bf16)
    for t in range(tiles):
        lanes = slice(t * LANES, (t + 1) * LANES)

        def term(c2):
            grad = dot_nt(da[t], bd[c2, t])
            weight = e_all[c2, :, lanes].astype(f32)
            return grad, weight * grad, weight

        own, dot_sum, e_sum = term(c)
        dw_s[...] = own

        def more(k, carry):
            _, x, y = term(lax.rem(c + k, nc))
            return carry[0] + x, carry[1] + y

        if nc <= 4:
            for k in range(1, nc):
                dot_sum, e_sum = more(k, (dot_sum, e_sum))
        else:
            dot_sum, e_sum = lax.fori_loop(1, nc, more, (dot_sum, e_sum))
        inverse = 1.0 / split_dot(e_sum, group)
        inv_t[:, lanes] = inverse
        diff = dw_s[...] - split_dot(dot_sum, group) * inverse
        d_send[:, :, lanes] = diff.astype(bf16).reshape(nb, ni, LANES)

    def d_copy(k, send):
        b2 = lax.rem(b + k, nb)
        return pltpu.make_async_remote_copy(
            src_ref=d_send.at[b2], dst_ref=d_recv.at[b if send else b2],
            send_sem=ds_sem.at[k], recv_sem=dr_sem.at[b if send else b2],
            device_id=(c, b2), device_id_type=MESH,
        )

    loop(nb - 1, lambda k: d_copy(k + 1, True).start())

    tokens = pl.ds(pl.multiple_of(c * nt, nt), nt)
    for t in range(tiles):
        lanes = slice(t * LANES, (t + 1) * LANES)
        scale = inv_t[tokens, lanes]

        def add(k, total):
            return total + dot(e_all[k, tokens, lanes], bd[k, t])

        total = jnp.zeros((nt, ns * LANES), f32)
        if nc <= 4:
            for k in range(nc):
                total = add(k, total)
        else:
            total = lax.fori_loop(0, nc, add, total)
        weight = (e_all[c, :, lanes].astype(f32) * inv_t[:, lanes]).astype(bf16)
        back = dot_tn(weight, da[t])
        for s in range(ns):
            span = slice(s * LANES, (s + 1) * LANES)
            avg_s[s * nt:(s + 1) * nt, lanes] = total[:, span] * scale
            picked = back[:nt, span]
            for h in range(1, per):
                picked = jnp.where(head_of == h, back[h * nt:(h + 1) * nt, span], picked)
            dv_s[s * nt:(s + 1) * nt, lanes] = picked.astype(bf16)
    gate = gate_s[...]
    gated = gate * avg_s[...]
    res_ref[...] = dot(gated.astype(bf16), wo_ref[...]).astype(bf16)
    d_pre = dg_s[...] * gated * (1.0 - gate)
    d_low = dot_nt(dv_s[...], wv_ref[...]) + dot_nt(d_pre.astype(bf16), wg_ref[...])
    dmsa_ref[...] = rows_backward(d_low, hat_s[...], rinv_s[...], mgain).astype(bf16)

    coeff = e_own[...] * inv_t[my_rows, :]
    total = d_send[b].astype(f32)
    for k in range(1, nb):
        d_copy(k, False).wait_recv()
        total = total + d_recv[lax.rem(b + k, nb)].astype(f32)
    d_logits = coeff * total
    wide = (d_logits[:, None, :] * same_j[None]).astype(bf16).reshape(ni * nt, chans)
    d_pair = dot_nt(wide, rep[...])
    dpair_ref[...] = rows_backward(d_pair, phat_s[...], prinv_s[...], pgain).astype(bf16)

    loop(nc - 1, lambda k: x_copy(k + 1).wait_send())

    def e_sent(k, _):
        e_copy(k, True).wait_send()
        return 0

    lax.fori_loop(1, nc * nb, e_sent, 0)
    loop(nb - 1, lambda k: d_copy(k + 1, True).wait_send())


def per_device(nc, nb, msa, pair, mgain, pgain, wv, wg, att, wo, cot):
    ns, nt, depth = msa.shape
    ni, nj, cz = pair.shape
    chans = wv.shape[1]
    nh = att.shape[1]
    tiles = chans // LANES
    n = nc * nt
    assert chans // nh == nt == nj and n == nb * ni and 2 * depth == LANES == cz
    rows = ns * nt
    vmem = pl.BlockSpec(memory_space=pltpu.VMEM)
    dma = pltpu.SemaphoreType.DMA
    outs = pl.pallas_call(
        functools.partial(kernel, nc, nb, ns, nt, ni, nh),
        out_shape=(
            jax.ShapeDtypeStruct((rows, depth), bf16),
            jax.ShapeDtypeStruct((rows, depth), bf16),
            jax.ShapeDtypeStruct((ni * nj, cz), bf16),
        ),
        in_specs=[vmem] * 9,
        out_specs=(vmem,) * 3,
        scratch_shapes=[
            pltpu.VMEM((nc, rows, LANES), bf16),
            pltpu.VMEM((nc, n, chans), bf16),
            pltpu.VMEM((nc, tiles, LANES, ns * LANES), bf16),
            pltpu.VMEM((tiles, n, ns * LANES), bf16),
            pltpu.VMEM((rows, chans), f32),
            pltpu.VMEM((rows, chans), f32),
            pltpu.VMEM((n, LANES), f32),
            pltpu.VMEM((n, chans), f32),
            pltpu.VMEM((rows, chans), f32),
            pltpu.VMEM((rows, chans), bf16),
            pltpu.VMEM((rows, depth), f32),
            pltpu.VMEM((rows, 1), f32),
            pltpu.VMEM((ni * nj, cz), f32),
            pltpu.VMEM((ni * nj, 1), f32),
            pltpu.VMEM((LANES, 2 * chans), bf16),
            pltpu.VMEM((chans, LANES), bf16),
            pltpu.VMEM((cz, chans), bf16),
            pltpu.VMEM((ni, chans), f32),
            pltpu.VMEM((nb, ni, chans), bf16),
            pltpu.VMEM((nb, ni, chans), bf16),
            dma((nc,)), dma((nc,)), dma((nc * nb,)), dma((nc * nb,)), dma((nb,)), dma((nb,)),
        ],
        compiler_params=pltpu.CompilerParams(
            collective_id=0, has_side_effects=True, vmem_limit_bytes=60 * 1024 * 1024
        ),
    )(
        msa.reshape(rows, depth), pair.reshape(ni * nj, cz),
        mgain.reshape(1, depth), pgain.reshape(1, cz), wv, wg, att, wo,
        cot.reshape(rows, depth),
    )
    return outs[0].reshape(msa.shape), outs[1].reshape(msa.shape), outs[2].reshape(pair.shape)


def solution(mesh):
    block = P("bulk", "col", None)
    return jax.shard_map(
        functools.partial(per_device, mesh.shape["col"], mesh.shape["bulk"]),
        mesh=mesh,
        in_specs=(block, block, P(), P(), P(), P(), P(), P(), block),
        out_specs=(block, block, block),
        check_vma=False,
    )
```

time: 106 us -> 28.9 us (0.27)
  blocking collectives: 45.3 us -> 0 us
  waiting for transfers between devices: 30.1 us -> 0 us
  Pallas kernels: 0 us -> 23 us
  between operations: 14.3 us -> 0.67 us
  matrix products: 5.12 us -> 0 us
  other arithmetic: 4.33 us -> 0 us
  local copies, waits for them, and re-layouts: 6.44 us -> 4.94 us
    reduce_scatter x2 -> x0, waiting for transfers between devices: 30 us -> none  [the longest x1 19.7 us: per_device(): lax.psum_scatter(weight_part.astype(jnp.bfloat16), 'bulk', scatter_dimens...]
    all_gather x2 -> x0, blocking collectives: 25.7 us -> none  [the longest x1 14.2 us: per_device(): weight_panel = lax.all_gather(weights_low, 'bulk', axis=1, tiled=True)]
    pallas_call x0 -> x1, Pallas kernels: none -> 23 us  [per_device(): pl.pallas_call(functools.partial(kernel, nc, nb, ns, nt, ni, nh), out_sha...]
    psum x2 -> x0, blocking collectives: 19.6 us -> none  [the longest x1 10.5 us: per_device(): lax.psum(jnp.sum(weights_low.astype(jnp.float32) * d_weights, axis=2), 'c...]
    dot_general x11 -> x0, matrix products: 5.12 us -> none  [the longest x1 1.18 us: per_device(): jnp.dot(switch_preimage_sensitivity, switch_single_form.T, precision=fine...]
    convert_element_type x5 -> x0, local copies, waits for them, and re-layouts: 2.62 us -> none  [the longest x2 1.05 us: per_device(): partial_low = partial_value.astype(jnp.bfloat16)]
    reduce_sum x5 -> x0, other arithmetic: 2.47 us -> none  [the longest x2 1.11 us: centred_sequences(): row_mean = jnp.mean(widened, axis=-1, keepdims=True)]
    convert_element_type x2 -> x0, other arithmetic: 1.84 us -> none  [the longest x1 1 us: per_device(): coupling_sensitivity = layernorm_reverse_mode(d_pair_low, pair_hat, pair_...]
  transfers between devices with their start and end apart: 2 -> 0, of which waited for: 2 -> 0; matrix products, arithmetic and copies ran while one was open for 3% -> 0% of each run, Pallas kernels for 0% -> 0%
where the time goes in v1:
time: 28.9 us; the launch traced here: 28.6 us
  Pallas kernels  23 us (80%)
  local copies, waits for them, and re-layouts  4.94 us (17%)
  between operations  0.67 us (2%)
    pallas_call x1, Pallas kernels, per_device(): pl.pallas_call(functools.partial(kernel, nc, nb, ns, nt, ni, nh), out_sha...  23 us
    unnamed x11, local copies, waits for them, and re-layouts  4.94 us

profile of v1, /device:TPU:0, one launch (start us, length us, event | category | flops | bytes accessed | tf_op | source)
XLA Modules:
  0.0 28.6 jit_solution(10259374117108636414)
XLA Ops:
  0.6 0.0 copy-start.2
  0.6 1.4 %copy.12.att_ref = bf16[128,8]{1,0:T(8,128)(2,1)} copy(bf16[128,8]{0,1:T(8,128)(2,1)} %param.15) | data formatting | bytes 4096 | tf_op args[6]
  2.0 0.0 copy-done.2
  2.0 0.7 %copy.13.wo_ref = bf16[256,64]{1,0:T(8,128)(2,1)} copy(bf16[256,64]{0,1:T(8,128)(2,1)S(1)} %copy-done.2) | data formatting | bytes 65536 | tf_op args[7]
  2.8 23.0 %shard_map.112 = (bf16[256,64]{1,0:T(8,128)(2,1)}, bf16[256,64]{1,0:T(8,128)(2,1)}, bf16[512,128]{1,0:T(8,128)(2,1)}) custom-call(bf16[256,64]{1,0:T(8,128)(2,1)} %bitcast.12, bf16[512,128]{1,0:T(8,128)(2,1)} %bitcast.8, f32[1,64]{1,0:T(1,128)} %bitcast.14, f32[1,128]{1,0:T(1,128)} %bitcast.15, bf16[64,256]{1,0:T(8,128)(2,1)} %wv_ref.1, ...), custom_call_target="tpu_custom_call" | custom-call | tf_op jit(solution)/shard_map/pallas_call | solution.py:285
  25.8 0.0 copy-start.1
  25.8 0.0 copy-start
  25.8 1.5 %copy.17 = bf16[8,32,64]{2,1,0:T(8,128)(2,1)} copy(bf16[8,32,64]{2,1,0:T(8,128)(2,1)} %bitcast.11) | data formatting | bytes 65536
  27.3 0.0 copy-done.1
  27.4 0.6 %copy.18 = bf16[8,32,64]{2,1,0:T(8,128)(2,1)} copy(bf16[8,32,64]{2,1,0:T(8,128)(2,1)S(1)} %bitcast.10) | data formatting | bytes 65536
  28.0 0.0 copy-done
  28.0 0.7 %copy.19 = bf16[16,32,128]{2,1,0:T(8,128)(2,1)} copy(bf16[16,32,128]{2,1,0:T(8,128)(2,1)S(1)} %bitcast.9) | data formatting | bytes 262144
Async XLA Ops:
  0.6 1.4 %copy-start.2 = (bf16[256,64]{0,1:T(8,128)(2,1)S(1)}, bf16[256,64]{0,1:T(8,128)(2,1)}, u32[]{:S(2)}) copy-start(bf16[256,64]{0,1:T(8,128)(2,1)} %param.16) | copy-start | bytes 98308
  25.8 1.5 %copy-start.1 = (bf16[256,64]{1,0:T(8,128)(2,1)S(1)}, bf16[256,64]{1,0:T(8,128)(2,1)}, u32[]{:S(2)}) copy-start(bf16[256,64]{1,0:T(8,128)(2,1)} %get-tuple-element.7) | copy-start | bytes 98308
  25.8 2.2 %copy-start = (bf16[512,128]{1,0:T(8,128)(2,1)S(1)}, bf16[512,128]{1,0:T(8,128)(2,1)}, u32[]{:S(2)}) copy-start(bf16[512,128]{1,0:T(8,128)(2,1)} %get-tuple-element.8) | copy-start | bytes 393220

commit v2 on v1

--- a/solution.py
+++ b/solution.py
@@ -55,11 +55,12 @@
 
 def kernel(
     nc, nb, ns, nt, ni, nh,
-    msa_ref, pair_ref, mgain_ref, pgain_ref, wv_ref, wg_ref, att_ref, wo_ref, cot_ref,
+    msa_in, pair_in, mgain_in, pgain_in, wv_in, wg_in, att_in, wo_in, cot_in,
     res_ref, dmsa_ref, dpair_ref,
     x_all, e_all, bd, da, gate_s, dg_s, dw_s, inv_t, avg_s, dv_s, hat_s, rinv_s,
     phat_s, prinv_s, wvg, wop, rep, e_own, d_send, d_recv,
-    xs_sem, xr_sem, es_sem, er_sem, ds_sem, dr_sem,
+    msa_ref, pair_ref, mgain_ref, pgain_ref, wv_ref, wg_ref, att_ref, wo_ref, cot_ref,
+    xs_sem, xr_sem, es_sem, er_sem, ds_sem, dr_sem, in_sem,
 ):
     c = lax.axis_index("col")
     b = lax.axis_index("bulk")
@@ -70,6 +71,15 @@
     per = LANES // hd
     n = nc * nt
 
+    pairs = (
+        (msa_in, msa_ref), (mgain_in, mgain_ref), (cot_in, cot_ref),
+        (pair_in, pair_ref), (pgain_in, pgain_ref), (att_in, att_ref),
+        (wv_in, wv_ref), (wg_in, wg_ref), (wo_in, wo_ref),
+    )
+    loads = [pltpu.make_async_copy(x, y, in_sem.at[k]) for k, (x, y) in enumerate(pairs)]
+    for load in loads:
+        load.start()
+
     barrier = pltpu.get_barrier_semaphore()
 
     def greet(k, _):
@@ -80,8 +90,9 @@
 
     lax.fori_loop(1, nc * nb, greet, 0)
 
+    for load in loads[:3]:
+        load.wait()
     mgain = mgain_ref[...]
-    pgain = pgain_ref[...]
     hat, rinv = normed_rows(msa_ref[...].astype(f32))
     hat_s[...] = hat
     rinv_s[...] = rinv
@@ -107,7 +118,10 @@
         lax.div(lax.broadcasted_iota(jnp.int32, (nh, chans), 1), nt)
         == lax.broadcasted_iota(jnp.int32, (nh, chans), 0)
     ).astype(bf16)
-    rep[...] = dot(att_ref[...], spread).astype(bf16)
+    for load in loads[3:6]:
+        load.wait()
+    pgain = pgain_ref[...]
+    rep[...] = dot_tn(att_ref[...], spread).astype(bf16)
     phat, prinv = normed_rows(pair_ref[...].astype(f32))
     phat_s[...] = phat
     prinv_s[...] = prinv
@@ -138,11 +152,13 @@
 
     lax.fori_loop(1, nc * nb, e_start, 0)
 
+    for load in loads[6:]:
+        load.wait()
     wvg[:depth, :chans] = wv_ref[...]
     wvg[:depth, chans:] = wg_ref[...]
     wvg[depth:, :] = jnp.zeros((depth, 2 * chans), bf16)
-    wop[:, :depth] = jnp.zeros((chans, depth), bf16)
-    wop[:, depth:] = wo_ref[...]
+    wop[:depth, :] = jnp.zeros((depth, chans), bf16)
+    wop[depth:, :] = wo_ref[...]
 
     head_of = lax.div(lax.broadcasted_iota(jnp.int32, (nt, LANES), 1), hd)
     head_masks = [(head_of == h).astype(f32).astype(bf16) for h in range(per)]
@@ -159,7 +175,7 @@
         both = dot(x, wvg[...])
         values = both[:, :chans].astype(bf16)
         gate = 1.0 / (1.0 + jnp.exp(-both[:, chans:]))
-        dg = dot_nt(x, wop[...])
+        dg = dot(x, wop[...])
         dav = (gate * dg).astype(bf16)
         if isinstance(k, int) and k == 0:
             gate_s[...] = gate
@@ -246,7 +262,7 @@
             dv_s[s * nt:(s + 1) * nt, lanes] = picked.astype(bf16)
     gate = gate_s[...]
     gated = gate * avg_s[...]
-    res_ref[...] = dot(gated.astype(bf16), wo_ref[...]).astype(bf16)
+    res_ref[...] = dot_nt(gated.astype(bf16), wo_ref[...]).astype(bf16)
     d_pre = dg_s[...] * gated * (1.0 - gate)
     d_low = dot_nt(dv_s[...], wv_ref[...]) + dot_nt(d_pre.astype(bf16), wg_ref[...])
     dmsa_ref[...] = rows_backward(d_low, hat_s[...], rinv_s[...], mgain).astype(bf16)
@@ -269,6 +285,15 @@
 
     lax.fori_loop(1, nc * nb, e_sent, 0)
     loop(nb - 1, lambda k: d_copy(k + 1, True).wait_send())
+
+
+def put_out(*refs):
+    sems = refs[-1]
+    copies = [pltpu.make_async_copy(refs[k], refs[k + 3], sems.at[k]) for k in range(3)]
+    for copy in copies:
+        copy.start()
+    for copy in copies:
+        copy.wait()
 
 
 def per_device(nc, nb, msa, pair, mgain, pgain, wv, wg, att, wo, cot):
@@ -285,11 +310,11 @@
     outs = pl.pallas_call(
         functools.partial(kernel, nc, nb, ns, nt, ni, nh),
         out_shape=(
-            jax.ShapeDtypeStruct((rows, depth), bf16),
-            jax.ShapeDtypeStruct((rows, depth), bf16),
-            jax.ShapeDtypeStruct((ni * nj, cz), bf16),
+            pltpu.VMEM((rows, depth), bf16),
+            pltpu.VMEM((rows, depth), bf16),
+            pltpu.VMEM((ni * nj, cz), bf16),
         ),
-        in_specs=[vmem] * 9,
+        in_specs=[pl.BlockSpec(memory_space=pltpu.HBM)] * 9,
         out_specs=(vmem,) * 3,
         scratch_shapes=[
             pltpu.VMEM((nc, rows, LANES), bf16),
@@ -307,21 +332,39 @@
             pltpu.VMEM((ni * nj, cz), f32),
             pltpu.VMEM((ni * nj, 1), f32),
             pltpu.VMEM((LANES, 2 * chans), bf16),
-            pltpu.VMEM((chans, LANES), bf16),
+            pltpu.VMEM((LANES, chans), bf16),
             pltpu.VMEM((cz, chans), bf16),
             pltpu.VMEM((ni, chans), f32),
             pltpu.VMEM((nb, ni, chans), bf16),
             pltpu.VMEM((nb, ni, chans), bf16),
+            pltpu.VMEM((rows, depth), bf16),
+            pltpu.VMEM((ni * nj, cz), bf16),
+            pltpu.VMEM((1, depth), f32),
+            pltpu.VMEM((1, cz), f32),
+            pltpu.VMEM(wv.shape, bf16),
+            pltpu.VMEM(wg.shape, bf16),
+            pltpu.VMEM((nh, cz), bf16),
+            pltpu.VMEM((depth, chans), bf16),
+            pltpu.VMEM((rows, depth), bf16),
             dma((nc,)), dma((nc,)), dma((nc * nb,)), dma((nc * nb,)), dma((nb,)), dma((nb,)),
+            dma((9,)),
         ],
         compiler_params=pltpu.CompilerParams(
-            collective_id=0, has_side_effects=True, vmem_limit_bytes=60 * 1024 * 1024
+            collective_id=0, has_side_effects=True, vmem_limit_bytes=62 * 1024 * 1024
         ),
     )(
         msa.reshape(rows, depth), pair.reshape(ni * nj, cz),
-        mgain.reshape(1, depth), pgain.reshape(1, cz), wv, wg, att, wo,
+        mgain.reshape(1, depth), pgain.reshape(1, cz), wv, wg, att.T, wo.T,
         cot.reshape(rows, depth),
     )
+    outs = pl.pallas_call(
+        put_out,
+        out_shape=tuple(jax.ShapeDtypeStruct(o.shape, o.dtype) for o in outs),
+        in_specs=[vmem] * 3,
+        out_specs=(pl.BlockSpec(memory_space=pltpu.HBM),) * 3,
+        scratch_shapes=[dma((3,))],
+        compiler_params=pltpu.CompilerParams(vmem_limit_bytes=4 * 1024 * 1024),
+    )(*outs)
     return outs[0].reshape(msa.shape), outs[1].reshape(msa.shape), outs[2].reshape(pair.shape)
 
 

time: 28.9 us -> 23.2 us (0.80)
  local copies, waits for them, and re-layouts: 4.94 us -> 0 us
  Pallas kernels: 23 us -> 22.4 us
    unnamed x11 -> x0, local copies, waits for them, and re-layouts: 4.94 us -> none
    pallas_call x1, Pallas kernels: 23 us -> 21.7 us  [per_device(): pl.pallas_call(functools.partial(kernel, nc, nb, ns, nt, ni, nh), out_sha...]
    pallas_call x0 -> x1, Pallas kernels: none -> 0.73 us  [per_device(): pl.pallas_call(put_out, out_shape=tuple((jax.ShapeDtypeStruct(o.shape, o....]
where the time goes in v2:
time: 23.2 us; the launch traced here: 23 us
  Pallas kernels  22.4 us (97%)
  between operations  0.64 us (3%)
    pallas_call x1, Pallas kernels, per_device(): pl.pallas_call(functools.partial(kernel, nc, nb, ns, nt, ni, nh), out_sha...  21.7 us
    pallas_call x1, Pallas kernels, per_device(): pl.pallas_call(put_out, out_shape=tuple((jax.ShapeDtypeStruct(o.shape, o....  0.73 us

profile of v2, /device:TPU:0, one launch (start us, length us, event | category | flops | bytes accessed | tf_op | source)
XLA Modules:
  0.0 23.0 jit_solution(14671566681259689368)
XLA Ops:
  0.6 21.7 %shard_map.112 = (bf16[256,64]{1,0:T(8,128)(2,1)S(1)}, bf16[256,64]{1,0:T(8,128)(2,1)S(1)}, bf16[512,128]{1,0:T(8,128)(2,1)S(1)}) custom-call(bf16[256,64]{1,0:T(8,128)(2,1)} %bitcast.11, bf16[512,128]{1,0:T(8,128)(2,1)} %bitcast.10, f32[1,64]{1,0:T(1,128)} %bitcast.15, f32[1,128]{1,0:T(1,128)} %bitcast.16, bf16[64,256]{1,0:T(8,128)(2,1)} %wv_in.1, ...), custom_call_target="tpu_custom_call" | custom-call | tf_op jit(solution)/shard_map/pallas_call | solution.py:310
  22.3 0.7 %shard_map.113 = (bf16[256,64]{1,0:T(8,128)(2,1)}, bf16[256,64]{1,0:T(8,128)(2,1)}, bf16[512,128]{1,0:T(8,128)(2,1)}) custom-call(bf16[256,64]{1,0:T(8,128)(2,1)S(1)} %get-tuple-element.9.refs_0_, bf16[256,64]{1,0:T(8,128)(2,1)S(1)} %get-tuple-element.10.refs_1_, bf16[512,128]{1,0:T(8,128)(2,1)S(1)} %get-tuple-element.11.refs_2_), custom_call_target="tpu_custom_call" | custom-call | tf_op jit(solution)/shard_map/pallas_call | solution.py:360

commit v3 on v2

--- a/solution.py
+++ b/solution.py
@@ -98,18 +98,6 @@
     rinv_s[...] = rinv
     x_all[c, :, :depth] = (hat * mgain).astype(bf16)
     x_all[c, :, depth:] = cot_ref[...]
-
-    pl.semaphore_wait(barrier, nc * nb - 1)
-
-    def x_copy(k):
-        c2 = lax.rem(c + k, nc)
-        return pltpu.make_async_remote_copy(
-            src_ref=x_all.at[c], dst_ref=x_all.at[c],
-            send_sem=xs_sem.at[k], recv_sem=xr_sem.at[c],
-            device_id=(c2, b), device_id_type=MESH,
-        )
-
-    loop(nc - 1, lambda k: x_copy(k + 1).start())
 
     lane = lax.broadcasted_iota(jnp.int32, (nt, chans), 1)
     row = lax.broadcasted_iota(jnp.int32, (nt, chans), 0)
@@ -132,25 +120,43 @@
     my_rows = pl.ds(pl.multiple_of(b * ni, ni), ni)
     e_all[c, my_rows, :] = e.astype(bf16)
 
-    def e_copy(k, send):
-        c2 = lax.rem(c + lax.div(k, nb), nc)
-        b2 = lax.rem(b + lax.rem(k, nb), nb)
-        if send:
-            block = e_all.at[c, my_rows]
-            slot = er_sem.at[c * nb + b]
-        else:
-            block = e_all.at[c2, pl.ds(pl.multiple_of(b2 * ni, ni), ni)]
-            slot = er_sem.at[c2 * nb + b2]
+    pl.semaphore_wait(barrier, nc * nb - 1)
+
+    def x_copy(k):
+        c2 = lax.rem(c + k, nc)
         return pltpu.make_async_remote_copy(
-            src_ref=block, dst_ref=block, send_sem=es_sem.at[k], recv_sem=slot,
-            device_id=(c2, b2), device_id_type=MESH,
+            src_ref=x_all.at[c], dst_ref=x_all.at[c],
+            send_sem=xs_sem.at[k], recv_sem=xr_sem.at[c],
+            device_id=(c2, b), device_id_type=MESH,
         )
 
+    loop(nc - 1, lambda k: x_copy(k + 1).start())
+
+    half = nb // 2
+    twin = b + 1 - 2 * lax.rem(b, 2)
+
+    def e_copy(k, first, slot, own=False, across=True):
+        c2 = lax.rem(c + lax.div(k, half), nc)
+        b2 = lax.rem(first + 2 * lax.rem(k, half), nb)
+        c3, b3 = (c, b) if own else (c2, b2)
+        block = e_all.at[c3, pl.ds(pl.multiple_of(b3 * ni, ni), ni)]
+        return pltpu.make_async_remote_copy(
+            src_ref=block, dst_ref=block, send_sem=es_sem.at[slot],
+            recv_sem=er_sem.at[c3 * nb + b3],
+            device_id=(c2, b2) if across else (c, twin), device_id_type=MESH,
+        )
+
     def e_start(k, _):
-        e_copy(k, True).start()
-        return 0
-
-    lax.fori_loop(1, nc * nb, e_start, 0)
+        e_copy(k, b, k, own=True).start()
+        return 0
+
+    def e_relay(k, _):
+        e_copy(k, b, nc * half + k).wait_recv()
+        e_copy(k, b, nc * half + k, across=False).start()
+        return 0
+
+    lax.fori_loop(1, nc * half, e_start, 0)
+    e_copy(0, b, nc * half, across=False).start()
 
     for load in loads[6:]:
         load.wait()
@@ -192,11 +198,20 @@
     chunk(0)
     loop(nc - 1, lambda k: chunk(k + 1))
 
+    lax.fori_loop(1, nc * half, e_relay, 0)
+
+    def grads(k):
+        c2 = lax.rem(c + k, nc)
+        for t in range(tiles):
+            dw_s[c2, :, t * LANES:(t + 1) * LANES] = dot_nt(da[t], bd[c2, t])
+
+    loop(nc, grads)
+
     def e_wait(k, _):
-        e_copy(k, False).wait_recv()
-        return 0
-
-    lax.fori_loop(1, nc * nb, e_wait, 0)
+        e_copy(k, twin, nc * half).wait_recv()
+        return 0
+
+    lax.fori_loop(0, nc * half, e_wait, 0)
 
     group = (
         lax.div(lax.broadcasted_iota(jnp.int32, (LANES, LANES), 1), hd)
@@ -206,15 +221,14 @@
         lanes = slice(t * LANES, (t + 1) * LANES)
 
         def term(c2):
-            grad = dot_nt(da[t], bd[c2, t])
+            grad = dw_s[c2, :, lanes]
             weight = e_all[c2, :, lanes].astype(f32)
-            return grad, weight * grad, weight
-
-        own, dot_sum, e_sum = term(c)
-        dw_s[...] = own
+            return weight * grad, weight
+
+        dot_sum, e_sum = term(c)
 
         def more(k, carry):
-            _, x, y = term(lax.rem(c + k, nc))
+            x, y = term(lax.rem(c + k, nc))
             return carry[0] + x, carry[1] + y
 
         if nc <= 4:
@@ -224,7 +238,7 @@
             dot_sum, e_sum = lax.fori_loop(1, nc, more, (dot_sum, e_sum))
         inverse = 1.0 / split_dot(e_sum, group)
         inv_t[:, lanes] = inverse
-        diff = dw_s[...] - split_dot(dot_sum, group) * inverse
+        diff = dw_s[c, :, lanes] - split_dot(dot_sum, group) * inverse
         d_send[:, :, lanes] = diff.astype(bf16).reshape(nb, ni, LANES)
 
     def d_copy(k, send):
@@ -280,10 +294,12 @@
     loop(nc - 1, lambda k: x_copy(k + 1).wait_send())
 
     def e_sent(k, _):
-        e_copy(k, True).wait_send()
-        return 0
-
-    lax.fori_loop(1, nc * nb, e_sent, 0)
+        e_copy(k, b, k, own=True).wait_send()
+        e_copy(k, b, nc * half + k, across=False).wait_send()
+        return 0
+
+    e_copy(0, b, nc * half, across=False).wait_send()
+    lax.fori_loop(1, nc * half, e_sent, 0)
     loop(nb - 1, lambda k: d_copy(k + 1, True).wait_send())
 
 
@@ -323,7 +339,7 @@
             pltpu.VMEM((tiles, n, ns * LANES), bf16),
             pltpu.VMEM((rows, chans), f32),
             pltpu.VMEM((rows, chans), f32),
-            pltpu.VMEM((n, LANES), f32),
+            pltpu.VMEM((nc, n, chans), f32),
             pltpu.VMEM((n, chans), f32),
             pltpu.VMEM((rows, chans), f32),
             pltpu.VMEM((rows, chans), bf16),

time: 23.2 us -> 20.9 us (0.901)
  Pallas kernels: 22.4 us -> 20.1 us
    pallas_call x1, Pallas kernels: 21.7 us -> 19.4 us  [per_device(): pl.pallas_call(functools.partial(kernel, nc, nb, ns, nt, ni, nh), out_sha...]
where the time goes in v3:
time: 20.9 us; the launch traced here: 20.7 us
  Pallas kernels  20.1 us (96%)
  between operations  0.64 us (3%)
    pallas_call x1, Pallas kernels, per_device(): pl.pallas_call(functools.partial(kernel, nc, nb, ns, nt, ni, nh), out_sha...  19.4 us
    pallas_call x1, Pallas kernels, per_device(): pl.pallas_call(put_out, out_shape=tuple((jax.ShapeDtypeStruct(o.shape, o....  0.73 us

profile of v3, /device:TPU:0, one launch (start us, length us, event | category | flops | bytes accessed | tf_op | source)
XLA Modules:
  0.0 20.7 jit_solution(6795287663913540633)
XLA Ops:
  0.6 19.4 %shard_map.112 = (bf16[256,64]{1,0:T(8,128)(2,1)S(1)}, bf16[256,64]{1,0:T(8,128)(2,1)S(1)}, bf16[512,128]{1,0:T(8,128)(2,1)S(1)}) custom-call(bf16[256,64]{1,0:T(8,128)(2,1)} %bitcast.11, bf16[512,128]{1,0:T(8,128)(2,1)} %bitcast.10, f32[1,64]{1,0:T(1,128)} %bitcast.15, f32[1,128]{1,0:T(1,128)} %bitcast.16, bf16[64,256]{1,0:T(8,128)(2,1)} %wv_in.1, ...), custom_call_target="tpu_custom_call" | custom-call | tf_op jit(solution)/shard_map/pallas_call | solution.py:326
  20.0 0.7 %shard_map.113 = (bf16[256,64]{1,0:T(8,128)(2,1)}, bf16[256,64]{1,0:T(8,128)(2,1)}, bf16[512,128]{1,0:T(8,128)(2,1)}) custom-call(bf16[256,64]{1,0:T(8,128)(2,1)S(1)} %get-tuple-element.9.refs_0_, bf16[256,64]{1,0:T(8,128)(2,1)S(1)} %get-tuple-element.10.refs_1_, bf16[512,128]{1,0:T(8,128)(2,1)S(1)} %get-tuple-element.11.refs_2_), custom_call_target="tpu_custom_call" | custom-call | tf_op jit(solution)/shard_map/pallas_call | solution.py:376
